TPU v7x, 32 devices: a whole 2x2x4 slice. The times are simulated.
32 devices in a mesh: pt: 8 (over y, x, core), md: 4 (over z).
Axes of the slice: x: 2, y: 2, z: 4, core: 2. Of those that a mesh axis runs over, the one named last changes fastest.
Arguments:
- grid_index: int32 [3, 8192], P(None, 'pt'), may hold values from 0 to 255, as said below
- wavenumbers: int32 [3, 32768], P(None, 'md'), may hold values from -16 to 15, as said below
- test_block: int32 [32768, 256], P('md'), may hold values from -64 to 63
- slab_counts: int32 [8], P('pt'), may hold values from 1 to 1024, as said below
Outputs:
- adjoint_sketch: float32 [32768, 512], P(('md', 'pt'))
Inputs may be any that keep to these rules, and one draw needn't show every extreme that they name: Each slab's live points are its first slab_counts slots; in every draw one slab is full with 1024. `grid_index`: every slot's point lies in the ball of radius 256 // 2 - 1 about the grid cell (128, 128, 128). `wavenumbers`: the columns are the 32 x 32 x 32 tensor grid of wavenumber triples, each exactly once, in some order.
All inputs are finite; a program needn't handle non-finite values.
Results may differ from a plain program's by a relative error of at most 0.002.
Values may be sent and summed in bfloat16 or wider, within the bound.
A program may use at most 192 MiB of HBM per device.

v0:
```python
import math

import jax
import jax.numpy as jnp
from jax import lax
from jax.sharding import PartitionSpec as P

M = 32768
PERIOD = 512


def phase_pair(coords, wave_cols, row_start, block, live_rows):
    rows = lax.dynamic_slice_in_dim(coords, row_start, block, 1)
    turns = (
        rows[0][:, None] * wave_cols[0][None, :]
        + rows[1][:, None] * wave_cols[1][None, :]
        + rows[2][:, None] * wave_cols[2][None, :]
    )
    turns = jnp.mod(turns, PERIOD)
    angles = turns.astype(jnp.float32) * (2.0 * math.pi / PERIOD)
    in_use = row_start + jnp.arange(block, dtype=jnp.int32) < live_rows
    tile_re = jnp.where(in_use[:, None], jnp.cos(angles), 0.0).astype(jnp.bfloat16)
    tile_im = jnp.where(in_use[:, None], jnp.sin(angles), 0.0).astype(jnp.bfloat16)
    return (tile_re, tile_im)


def adjoint_piece(tile_re, tile_im, rows, width):
    dims = (((0,), (0,)), ((), ()))
    from_re = lax.dot_general(tile_re, rows, dims, preferred_element_type=jnp.float32)
    from_im = lax.dot_general(tile_im, rows, dims, preferred_element_type=jnp.float32)
    return jnp.concatenate(
        [from_re[:, :width] + from_im[:, width:], from_re[:, width:] - from_im[:, :width]], axis=1
    )


def per_device(grid_index, wavenumbers, test_block, slab_counts):
    capacity = grid_index.shape[1]
    width = test_block.shape[1]
    block = min(512, capacity)
    test_bf = test_block.astype(jnp.bfloat16)
    y_scale = 1.0 / (32.0 * math.sqrt(M))
    w_scale = 1.0 / math.sqrt(capacity * lax.axis_size("pt"))
    live_rows = slab_counts[0]
    block_count = (live_rows + block - 1) // block
    modes_local = wavenumbers.shape[1]

    def sketch_step(step_index, summed):
        row_start = step_index * block
        tile_re, tile_im = phase_pair(grid_index, wavenumbers, row_start, block, live_rows)
        part = jnp.concatenate(
            [
                jnp.dot(tile_re, test_bf, preferred_element_type=jnp.float32),
                jnp.dot(tile_im, test_bf, preferred_element_type=jnp.float32),
            ],
            axis=1,
        )
        return lax.dynamic_update_slice_in_dim(summed, part, row_start, 0)

    partial_value = lax.fori_loop(
        0, block_count, sketch_step, jnp.zeros((capacity, 2 * width), jnp.float32)
    )
    sketch = (lax.psum(partial_value, "md") * y_scale).astype(jnp.bfloat16)

    def fresh_step(step_index, summed):
        row_start = step_index * block
        tile_re, tile_im = phase_pair(grid_index, wavenumbers, row_start, block, live_rows)
        rows = lax.dynamic_slice_in_dim(sketch, row_start, block, 0)
        return summed + adjoint_piece(tile_re, tile_im, rows, width)

    summed = lax.fori_loop(
        0,
        block_count,
        fresh_step,
        jnp.zeros(
            (modes_local // lax.axis_size("pt") * lax.axis_size("pt"), 2 * width), jnp.float32
        ),
    )
    return lax.psum_scatter(summed * w_scale, "pt", scatter_dimension=0, tiled=True)


def solution(mesh):
    placed = (P(None, "pt"), P(None, "md"), P("md", None), P("pt"))
    return jax.shard_map(
        per_device, mesh=mesh, in_specs=placed, out_specs=P(("md", "pt"), None), check_vma=False
    )
```

profile of v0, /device:TPU:16, one launch (start us, length us, event | category | flops | bytes accessed | tf_op | source)
XLA Modules:
  0.0 942.5 jit_solution(14429266977389757838)
XLA Ops:
  7.2 6.0 convert_element_type.42
  13.2 1.6 broadcast_in_dim.53.clone
  14.8 141.9 %while.24 = (s32[]{:T(128)}, f32[1024,512]{1,0:T(8,128)}, s32[]{:T(128)}, s32[]{:T(128)}, s32[3,1024]{1,0:T(4,128)}, /*index=5*/s32[3,8192]{1,0:T(4,128)}, bf16[...) while((s32[]{:T(128)}, f32[1024,512]{1,0:T(8,128)}, ...), condition=%wide.region_1.2_spmd, body=%wide.region_0.1_spmd.sunk | while | flops 4463002624 | bytes 66479860 | solution.py:59
  14.8 0.8 add_compare_fusion.4
  15.6 1.0 constant_dynamic-slice_fusion.4
  16.6 1.2 fusion.80
  17.8 65.0 %select_convert_fusion.25 = bf16[512,8192]{1,0:T(8,128)(2,1)S(1)} fusion(s32[8192]{0:T(1024)S(1)} %bitcast.60, s32[512]{0:T(512)S(1)} %bitcast.74, s32[8192]{0:T(1024)S(1)} %bitcast.62, s32[512]{0:T(512)S(1)} %bitcast.72, s32[8192]{0:T(1024)S(1)} %bitcast.58, s32[512]{0:T(512)S(1)} %bitcast.70, pred[512]{0:T(512)(128)(4,1)S(1)} %add_compare_fusion.4), kind=kLoop, calls=%fused_computation.7.clone.clone.1.clone.1 | loop fusion | flops 83886080 | bytes 8493568 | tf_op jit(solution)/shard_map/while/body/dot_general | solution.py:52
  82.8 4.6 fusion.82
  87.4 65.5 %select_convert_fusion.24 = bf16[512,8192]{1,0:T(8,128)(2,1)S(1)} fusion(s32[8192]{0:T(1024)S(1)} %bitcast.61, s32[512]{0:T(512)S(1)} %bitcast.75, s32[8192]{0:T(1024)S(1)} %bitcast.63, s32[512]{0:T(512)S(1)} %bitcast.73, s32[8192]{0:T(1024)S(1)} %bitcast.59, s32[512]{0:T(512)S(1)} %bitcast.71, pred[512]{0:T(512)(128)(4,1)S(1)} %add_compare_fusion.4), kind=kLoop, calls=%fused_computation.6.clone.clone.1.clone.1 | loop fusion | flops 83886080 | bytes 8493568 | tf_op jit(solution)/shard_map/while/body/dot_general | solution.py:53
  152.9 2.4 fusion.81
  155.7 1.0 constant_dynamic-update-slice_fusion.2
  156.8 227.5 %all-reduce.2.cloned.1.call-done = f32[1024,512]{1,0:T(8,128)} async-done(((f32[1024,512]{1,0:T(8,128)}), f32[1024,512]{1,0:T(8,128)}) %all-reduce.2.cloned.1.call-update) | async-done | bytes 2097168 | tf_op jit(solution)/shard_map/psum | solution.py:62
  384.3 1.9 multiply_convert_fusion
  386.2 7.8 broadcast_in_dim.52
  393.9 199.6 %while.25 = (s32[]{:T(128)}, f32[8192,512]{0,1:T(8,128)}, s32[]{:T(128)}, s32[]{:T(128)}, s32[3,1024]{1,0:T(4,128)}, /*index=5*/s32[3,8192]{1,0:T(4,128)S(1)}, b...) while((s32[]{:T(128)}, f32[8192,512]{0,1:T(8,128)}, ...), condition=%wide.region_4.5_spmd, body=%wide.region_3.4_spmd.sunk | while | flops 8770290688 | bytes 137783024 | solution.py:70
  405.8 0.7 add_compare_fusion.5
  406.5 0.9 constant_dynamic-slice_fusion.5
  407.6 67.4 %fusion.89 = f32[8192,512]{0,1:T(8,128)} fusion(s32[8192]{0:T(1024)S(1)} %bitcast.66, s32[512]{0:T(512)S(1)} %bitcast.80, s32[8192]{0:T(1024)S(1)} %bitcast.68, s32[512]{0:T(512)S(1)} %bitcast.78, s32[8192]{0:T(1024)S(1)} %bitcast.64, s32[512]{0:T(512)S(1)} %bitcast.76, pred[512]{0:T(512)(128)(4,1)S(1)} %add_compare_fusion.5, ...), kind=kOutput, calls=%fused_computation.37.clone.3 | convolution fusion | flops 4378853376 | bytes 17406464 | tf_op jit(solution)/shard_map/while/body/dot_general | solution.py:29
  474.9 81.0 %fusion.87 = f32[8192,512]{0,1:T(8,128)} fusion(s32[8192]{0:T(1024)S(1)} %bitcast.67, s32[512]{0:T(512)S(1)} %bitcast.81, s32[8192]{0:T(1024)S(1)} %bitcast.69, s32[512]{0:T(512)S(1)} %bitcast.79, s32[8192]{0:T(1024)S(1)} %bitcast.65, s32[512]{0:T(512)S(1)} %bitcast.77, pred[512]{0:T(512)(128)(4,1)S(1)} %add_compare_fusion.5, ...), kind=kOutput, calls=%fused_computation.38.clone.3 | convolution fusion | flops 4378853376 | bytes 17406464 | tf_op jit(solution)/shard_map/while/body/dot_general | solution.py:30
  556.0 18.0 %slice_add_fusion.2 = (f32[8192,256]{0,1:T(8,128)}, f32[8192,256]{0,1:T(8,128)}) fusion(f32[8192,512]{0,1:T(8,128)} %fusion.87, f32[8192,512]{0,1:T(8,128)} %fusion.89), kind=kLoop, calls=%fused_computation.40.clone.1 | loop fusion | flops 4194304 | bytes 50331648 | tf_op jit(solution)/shard_map/while/body/add | solution.py:32
  574.0 17.2 %maximum_add_fusion.2 = f32[8192,512]{0,1:T(8,128)} fusion(f32[8192,512]{0,1:T(8,128)} %get-tuple-element.404, f32[8192,256]{0,1:T(8,128)} %get-tuple-element.349, f32[8192,256]{0,1:T(8,128)} %get-tuple-element.350), kind=kLoop, calls=%fused_computation.34.clone.1 | loop fusion | flops 8388608 | bytes 50331648 | tf_op jit(solution)/shard_map/while/body/add | solution.py:68
  593.5 17.4 %copy.6 = f32[8192,512]{1,0:T(8,128)} copy(f32[8192,512]{0,1:T(8,128)} %get-tuple-element.192) | data formatting | bytes 33554432 | tf_op jit(solution)/shard_map/while | solution.py:70
  611.0 11.7 %broadcast_multiply_fusion = f32[8192,512]{1,0:T(8,128)} fusion(f32[8192,512]{1,0:T(8,128)} %copy.6), kind=kLoop, calls=%fused_computation.59 | loop fusion | flops 4194304 | bytes 33554432 | tf_op jit(solution)/shard_map/mul | solution.py:78
  622.7 312.5 %reduce-scatter.2.cloned.1.call-done = f32[1024,512]{1,0:T(8,128)} async-done(((f32[8192,512]{1,0:T(8,128)}), f32[1024,512]{1,0:T(8,128)}) %reduce-scatter.2.cloned.1.call-update) | async-done | bytes 2097168 | tf_op jit(solution)/shard_map/reduce_scatter | solution.py:78
  (13 shorter events, 0.6 us)
Async XLA Ops:
  6.5 377.7 %all-reduce.2.cloned.1.call-start = ((), (), s32[]{:S(2)}) async-start(), calls=%async_computation.1 | async-start | bytes 4194304 | tf_op jit(solution)/shard_map/psum | solution.py:62
  14.8 138.1 %copy-start.1 = (bf16[8192,256]{1,0:T(8,128)(2,1)S(1)}, bf16[8192,256]{1,0:T(8,128)(2,1)}, u32[]{:S(2)}) copy-start(bf16[8192,256]{1,0:T(8,128)(2,1)} %get-tuple-element.383) | copy-start | bytes 12582916 | tf_op jit(solution)/shard_map/while
  156.7 237.2 %copy-start = (s32[3,8192]{1,0:T(4,128)S(1)}, s32[3,8192]{1,0:T(4,128)}, u32[]{:S(2)}) copy-start(s32[3,8192]{1,0:T(4,128)} %get-tuple-element.435) | copy-start | bytes 294916
  156.7 778.5 %reduce-scatter.2.cloned.1.call-start = ((), (), s32[]{:S(2)}) async-start(), calls=%async_computation.2 | async-start | bytes 18874368 | tf_op jit(solution)/shard_map/reduce_scatter | solution.py:78
Sparse Core Ops, SparseCore 0:
  156.9 227.3 all-reduce.1
  622.9 312.3 reduce-scatter.1
where the time goes:
time: 946 us; the launch traced here: 942 us
  waiting for transfers between devices  540 us (57%)
  other arithmetic  187 us (20%)
  matrix products  155 us (16%)
  local copies, waits for them, and re-layouts  31.4 us (3%)
  loops' own time  14.4 us (2%)
  between operations  14.4 us (2%)
    reduce_scatter x1, waiting for transfers between devices, per_device(): lax.psum_scatter(summed * w_scale, 'pt', scatter_dimension=0, tiled=True)  313 us
    psum x1, waiting for transfers between devices, per_device(): sketch = (lax.psum(partial_value, 'md') * y_scale).astype(jnp.bfloat16)  228 us
    dot_general x1, matrix products, adjoint_piece(): lax.dot_general(tile_im, rows, dims, preferred_element_type=jnp.float32)  81 us
    dot_general x1, matrix products, adjoint_piece(): lax.dot_general(tile_re, rows, dims, preferred_element_type=jnp.float32)  67.4 us
    dot_general x1, other arithmetic, sketch_step(): jnp.dot(tile_im, test_bf, preferred_element_type=jnp.float32)  65.5 us
    dot_general x1, other arithmetic, sketch_step(): jnp.dot(tile_re, test_bf, preferred_element_type=jnp.float32)  65 us
  transfers between devices with their start and end apart: 2, of which 2 were waited for; matrix products, arithmetic and copies ran while one was open for 0% of the time, Pallas kernels for 0%

commit v1 on v0

v1 whole, which is shorter than its diff:
```python
import functools
import math

import jax
import jax.numpy as jnp
from jax import lax
from jax.experimental import pallas as pl
from jax.experimental.pallas import tpu as pltpu
from jax.sharding import PartitionSpec as P

M = 32768
PERIOD = 512
DEPTH = 128
TILE = 256
STRIP = 32

S = (4.4428679, -7.3074434, 3.59478791, -0.78437358)
C = (1.41420408, -6.97764202, 5.71523797, -1.72834735)


def phases(whole_turns):
    r = whole_turns - jnp.round(whole_turns)
    z = r * r
    s = (((S[3] * z + S[2]) * z + S[1]) * z + S[0]) * r
    c = ((C[3] * z + C[2]) * z + C[1]) * z + C[0]
    return 1.0 - s * s, s * c


def sketch_kernel(count_ref, points_ref, waves_ref, test_ref, out_ref, turns_ref, lhs_ref):
    rows, width = out_ref.shape[0], test_ref.shape[1]

    @pl.when(pl.program_id(0) == 0)
    def _():
        out_ref[...] = jnp.zeros_like(out_ref)

    def block(index, carry):
        first = pl.multiple_of(index * TILE, TILE)
        total = None
        for k in range(test_ref.shape[0] // TILE):
            cols = pl.ds(k * TILE, TILE)
            turns_ref[k] = jnp.dot(
                points_ref[pl.ds(first, TILE), :], waves_ref[:, cols], preferred_element_type=jnp.float32
            )
            for j in range(TILE // STRIP):
                re, im = phases(turns_ref[k, pl.ds(j * STRIP, STRIP), :])
                lhs_ref[k, pl.ds(j * STRIP, STRIP), :] = re.astype(jnp.bfloat16)
                lhs_ref[k, pl.ds(TILE + j * STRIP, STRIP), :] = im.astype(jnp.bfloat16)
            test = test_ref[cols, :].astype(jnp.float32).astype(jnp.bfloat16)
            part = jnp.dot(lhs_ref[k], test, preferred_element_type=jnp.float32)
            total = part if total is None else total + part
        out_ref[pl.ds(first, TILE), pl.ds(0, width)] += total[:TILE]
        out_ref[pl.ds(first, TILE), pl.ds(width, width)] += total[TILE:]
        return carry

    lax.fori_loop(0, (count_ref[0] + TILE - 1) // TILE, block, 0)


def adjoint_kernel(scale, counts_ref, waves_ref, points_ref, sketch_ref, out_ref, turns_ref, lhs_ref, rhs_ref):
    modes, width = out_ref.shape[0], sketch_ref.shape[1] // 2
    slab = pl.program_id(0)

    @pl.when(slab == 0)
    def _():
        out_ref[...] = jnp.zeros_like(out_ref)

    def block(index, carry):
        first = pl.multiple_of(index * TILE, TILE)
        rhs_ref[pl.ds(0, TILE), :] = sketch_ref[pl.ds(first, TILE), :]
        rhs_ref[pl.ds(TILE, TILE), pl.ds(0, width)] = sketch_ref[pl.ds(first, TILE), pl.ds(width, width)]
        rhs_ref[pl.ds(TILE, TILE), pl.ds(width, width)] = -sketch_ref[pl.ds(first, TILE), pl.ds(0, width)]
        for k in range(modes // TILE):
            rows = pl.ds(k * TILE, TILE)
            turns_ref[k] = jnp.dot(
                waves_ref[rows, :], points_ref[:, pl.ds(first, TILE)], preferred_element_type=jnp.float32
            )
            for j in range(TILE // STRIP):
                re, im = phases(turns_ref[k, pl.ds(j * STRIP, STRIP), :])
                lhs_ref[k, pl.ds(j * STRIP, STRIP), pl.ds(0, TILE)] = re.astype(jnp.bfloat16)
                lhs_ref[k, pl.ds(j * STRIP, STRIP), pl.ds(TILE, TILE)] = im.astype(jnp.bfloat16)
            out_ref[rows, :] += jnp.dot(lhs_ref[k], rhs_ref[...], preferred_element_type=jnp.float32)
        return carry

    lax.fori_loop(0, (counts_ref[slab] + TILE - 1) // TILE, block, 0)

    @pl.when(slab == pl.num_programs(0) - 1)
    def _():
        out_ref[...] = out_ref[...] * scale


def padded(rows, factor):
    rows = rows.astype(jnp.float32) * factor
    return jnp.pad(rows, ((0, DEPTH - rows.shape[0]), (0, 0))).astype(jnp.bfloat16)


def sketch_part(count, points, waves, test_block):
    rows, modes, width = points.shape[0], waves.shape[1], test_block.shape[1]
    step = 1024
    return pl.pallas_call(
        sketch_kernel,
        out_shape=jax.ShapeDtypeStruct((rows, 2 * width), jnp.float32),
        grid=(modes // step,),
        in_specs=[
            pl.BlockSpec(memory_space=pltpu.SMEM),
            pl.BlockSpec((rows, DEPTH), lambda m: (0, 0)),
            pl.BlockSpec((DEPTH, step), lambda m: (0, m)),
            pl.BlockSpec((step, width), lambda m: (m, 0)),
        ],
        out_specs=pl.BlockSpec((rows, 2 * width), lambda m: (0, 0)),
        scratch_shapes=[
            pltpu.VMEM((step // TILE, TILE, TILE), jnp.float32),
            pltpu.VMEM((step // TILE, 2 * TILE, TILE), jnp.bfloat16),
        ],
        compiler_params=pltpu.CompilerParams(vmem_limit_bytes=40 * 2**20),
        cost_estimate=pl.CostEstimate(
            flops=4 * rows * modes * width, bytes_accessed=4 * modes * width, transcendentals=0
        ),
    )(count, points, waves, test_block)


def adjoint_part(scale, counts, waves, points, sketch, capacity):
    modes, slots, width = waves.shape[0], points.shape[1], sketch.shape[1]
    return pl.pallas_call(
        functools.partial(adjoint_kernel, scale),
        out_shape=jax.ShapeDtypeStruct((modes, width), jnp.float32),
        grid=(slots // capacity,),
        in_specs=[
            pl.BlockSpec(memory_space=pltpu.SMEM),
            pl.BlockSpec((modes, DEPTH), lambda p: (0, 0)),
            pl.BlockSpec((DEPTH, capacity), lambda p: (0, p)),
            pl.BlockSpec((capacity, width), lambda p: (p, 0)),
        ],
        out_specs=pl.BlockSpec((modes, width), lambda p: (0, 0)),
        scratch_shapes=[
            pltpu.VMEM((modes // TILE, TILE, TILE), jnp.float32),
            pltpu.VMEM((modes // TILE, TILE, 2 * TILE), jnp.bfloat16),
            pltpu.VMEM((2 * TILE, width), jnp.bfloat16),
        ],
        compiler_params=pltpu.CompilerParams(vmem_limit_bytes=40 * 2**20),
        cost_estimate=pl.CostEstimate(
            flops=4 * modes * slots * width, bytes_accessed=2 * slots * width, transcendentals=0
        ),
    )(counts, waves, points, sketch)


def per_device(grid_index, wavenumbers, test_block, slab_counts):
    capacity = grid_index.shape[1]
    n_pt = lax.axis_size("pt")
    y_scale = 1.0 / (32.0 * math.sqrt(M))
    w_scale = 1.0 / math.sqrt(capacity * n_pt)
    counts = lax.all_gather(slab_counts, "pt", tiled=True)
    all_points = lax.all_gather(grid_index, "pt", axis=1, tiled=True)
    points = padded(grid_index, 1.0)
    waves = padded(wavenumbers, 1.0 / PERIOD)
    partial_value = sketch_part(slab_counts, points.T, waves, test_block)
    quarter = lax.psum_scatter(partial_value, "md", scatter_dimension=0, tiled=True)
    rows = quarter.shape[0]
    slot = lax.axis_index("md") * rows + jnp.arange(rows, dtype=jnp.int32)
    quarter = jnp.where((slot < slab_counts[0])[:, None], quarter * y_scale, 0.0).astype(jnp.bfloat16)
    sketch = lax.all_gather(quarter, ("pt", "md"), tiled=True)
    own = wavenumbers.shape[1] // n_pt
    mine = lax.dynamic_slice_in_dim(waves, lax.axis_index("pt") * own, own, 1)
    return adjoint_part(w_scale, counts, mine.T, padded(all_points, 1.0), sketch, capacity)


def solution(mesh):
    placed = (P(None, "pt"), P(None, "md"), P("md", None), P("pt"))
    return jax.shard_map(
        per_device, mesh=mesh, in_specs=placed, out_specs=P(("md", "pt"), None), check_vma=False
    )
```

time: 946 us -> 230 us (0.24)
  waiting for transfers between devices: 540 us -> 122 us
  other arithmetic: 187 us -> 3.57 us
  matrix products: 155 us -> 0 us
  Pallas kernels: 0 us -> 58.5 us
  local copies, waits for them, and re-layouts: 31.4 us -> 11.9 us
  blocking collectives: 0 us -> 16.5 us
  loops' own time: 14.4 us -> 0 us
    reduce_scatter x1, waiting for transfers between devices: 313 us -> 62.6 us  [per_device(): lax.psum_scatter(partial_value, 'md', scatter_dimension=0, tiled=True)]
    psum x1 -> x0, waiting for transfers between devices: 228 us -> none  [per_device(): sketch = (lax.psum(partial_value, 'md') * y_scale).astype(jnp.bfloat16)]
    dot_general x4 -> x0, matrix products: 155 us -> none  [the longest x1 81 us: adjoint_piece(): lax.dot_general(tile_im, rows, dims, preferred_element_type=jnp.float32)]
    dot_general x2 -> x0, other arithmetic: 130 us -> none  [the longest x1 65.5 us: sketch_step(): jnp.dot(tile_im, test_bf, preferred_element_type=jnp.float32)]
    all_gather x0 -> x1, waiting for transfers between devices: none -> 59.5 us  [per_device(): sketch = lax.all_gather(quarter, ('pt', 'md'), tiled=True)]
    pallas_call x0 -> x2, Pallas kernels: none -> 58.5 us  [the longest x1 37.6 us: adjoint_part(): pl.pallas_call(functools.partial(adjoint_kernel, scale), out_shape=jax.Sh...]
    add x2 -> x0, other arithmetic: 35.2 us -> none  [the longest x1 18 us: adjoint_piece(): from_re[:, :width] + from_im[:, width:]]
    while x3 -> x0, local copies, waits for them, and re-layouts: 17.5 us -> none  [the longest x1 17.4 us: per_device(): lax.fori_loop(0, block_count, fresh_step, jnp.zeros((modes_local // lax.a...]
  transfers between devices with their start and end apart: 2 -> 2, of which waited for: 2 -> 2; matrix products, arithmetic and copies ran while one was open for 0% -> 1% of each run, Pallas kernels for 0% -> 0%
where the time goes in v1:
time: 230 us; the launch traced here: 227 us
  waiting for transfers between devices  122 us (53%)
  Pallas kernels  58.5 us (25%)
  blocking collectives  16.5 us (7%)
  between operations  14.1 us (6%)
  local copies, waits for them, and re-layouts  11.9 us (5%)
  other arithmetic  3.57 us (2%)
    reduce_scatter x1, waiting for transfers between devices, per_device(): lax.psum_scatter(partial_value, 'md', scatter_dimension=0, tiled=True)  62.6 us
    all_gather x1, waiting for transfers between devices, per_device(): sketch = lax.all_gather(quarter, ('pt', 'md'), tiled=True)  59.5 us
    pallas_call x1, Pallas kernels, adjoint_part(): pl.pallas_call(functools.partial(adjoint_kernel, scale), out_shape=jax.Sh...  37.6 us
    pallas_call x1, Pallas kernels, sketch_part(): pl.pallas_call(sketch_kernel, out_shape=jax.ShapeDtypeStruct((rows, 2 * w...  20.9 us
    unnamed x14, local copies, waits for them, and re-layouts  9.1 us
    all_gather x1, blocking collectives, per_device(): all_points = lax.all_gather(grid_index, 'pt', axis=1, tiled=True)  8.55 us
    unnamed x1, blocking collectives  7.95 us
  transfers between devices with their start and end apart: 2, of which 2 were waited for; matrix products, arithmetic and copies ran while one was open for 1% of the time, Pallas kernels for 0%

profile of v1, /device:TPU:16, one launch (start us, length us, event | category | flops | bytes accessed | tf_op | source)
XLA Modules:
  0.0 226.7 jit_solution(14875343979152457388)
XLA Ops:
  7.2 0.7 convert_convert_fusion.1
  7.9 0.9 multiply_convert_fusion
  8.9 0.2 copy.10
  9.1 0.1 pad_bitcast_fusion.points_ref
  9.1 1.1 copy.9
  10.2 0.9 copy.12
  11.1 0.2 pad.14.clone.waves_ref
  11.3 0.2 copy-done.2
  11.5 3.4 %copy-done = s32[8192,256]{1,0:T(8,128)S(1)} copy-done((s32[8192,256]{1,0:T(8,128)S(1)}, s32[8192,256]{1,0:T(8,128)}, u32[]{:S(2)}) %copy-start) | copy-done | bytes 8388632
  14.9 20.9 %shard_map.46 = f32[1024,512]{1,0:T(8,128)} custom-call(s32[1]{0:T(128)} %copy.14.count_ref, bf16[1024,128]{1,0:T(8,128)(2,1)S(1)} %pad_bitcast_fusion.points_ref, bf16[128,8192]{1,0:T(8,128)(2,1)S(1)} %pad.14.clone.waves_ref, s32[8192,256]{1,0:T(8,128)S(1)} %copy-done), custom_call_target="tpu_custom_call" | custom-call | flops 8589934592 | bytes 8388608 | tf_op jit(solution)/shard_map/pallas_call | solution.py:98
  35.9 0.0 reduce-scatter.2.cloned.1.call-update
  35.9 0.0 all-gather.2.cloned.1.call-start
  35.9 62.6 %reduce-scatter.2.cloned.1.call-done = f32[256,512]{1,0:T(8,128)} async-done(((f32[1024,512]{1,0:T(8,128)}), f32[256,512]{1,0:T(8,128)}) %reduce-scatter.2.cloned.1.call-update) | async-done | bytes 524304 | tf_op jit(solution)/shard_map/reduce_scatter | solution.py:155
  98.5 1.9 select_convert_fusion
  100.4 0.0 all-gather.2.cloned.1.call-update
  100.4 0.6 dynamic-slice
  101.0 0.7 dynamic-update-slice
  101.7 8.0 %all-reduce.3.counts_ref = s32[8]{0:T(128)S(1)} all-reduce(s32[8]{0:T(128)S(1)} %dynamic-update-slice), channel_id=1, replica_groups=mesh['pt'=8,'md'=4] {'pt'}, use_global_device_ids=true, to_apply=%add.3 | all-reduce | flops 8 | bytes 64
  109.6 8.5 %all_gather.10 = s32[3,8192]{1,0:T(4,128)S(1)} all-gather(s32[3,1024]{1,0:T(4,128)S(1)} %copy-done.3), channel_id=1, replica_groups=mesh['pt'=8,'md'=4] {'pt'}, dimensions={1}, use_global_device_ids=true | all-gather | bytes 110592 | tf_op jit(solution)/shard_map/all_gather | solution.py:151
  118.2 0.2 pad.15.points_ref
  118.4 1.0 dynamic-slice_bitcast_fusion.waves_ref
  119.4 59.5 %all-gather.2.cloned.1.call-done.sketch_ref = bf16[8192,512]{1,0:T(8,128)(2,1)} async-done(((bf16[256,512]{1,0:T(8,128)(2,1)}), bf16[8192,512]{1,0:T(8,128)(2,1)}) %all-gather.2.cloned.1.call-update) | async-done | bytes 8388624 | tf_op jit(solution)/shard_map/all_gather | solution.py:159
  178.9 3.4 %copy-done.1 = bf16[8192,512]{1,0:T(8,128)(2,1)S(1)} copy-done((bf16[8192,512]{1,0:T(8,128)(2,1)S(1)}, bf16[8192,512]{1,0:T(8,128)(2,1)}, u32[]{:S(2)}) %copy-start.1) | copy-done | bytes 8388632
  182.3 37.6 %shard_map.47 = f32[1024,512]{1,0:T(8,128)} custom-call(s32[8]{0:T(128)S(1)} %all-reduce.3.counts_ref, bf16[1024,128]{1,0:T(8,128)(2,1)S(1)} %dynamic-slice_bitcast_fusion.waves_ref, bf16[128,8192]{1,0:T(8,128)(2,1)S(1)} %pad.15.points_ref, bf16[8192,512]{1,0:T(8,128)(2,1)S(1)} %copy-done.1), custom_call_target="tpu_custom_call" | custom-call | flops 17179869184 | bytes 8388608 | tf_op jit(solution)/shard_map/pallas_call | solution.py:122
  (11 shorter events, 0.1 us)
Async XLA Ops:
  6.5 92.0 %reduce-scatter.2.cloned.1.call-start = ((), (), s32[]{:S(2)}) async-start(), calls=%async_computation.1 | async-start | bytes 2621440 | tf_op jit(solution)/shard_map/reduce_scatter | solution.py:155
  10.2 1.3 copy-start.2
  11.5 3.4 %copy-start = (s32[8192,256]{1,0:T(8,128)S(1)}, s32[8192,256]{1,0:T(8,128)}, u32[]{:S(2)}) copy-start(s32[8192,256]{1,0:T(8,128)} %test_ref.1) | copy-start | bytes 25165828
  35.9 64.6 %copy-start.4 = (u32[32]{0:T(128)S(1)}, u32[32]{0:T(128)}, u32[]{:S(2)}) copy-start(u32[32]{0:T(128)} %constant.35) | copy-start | bytes 388
  35.9 73.8 %copy-start.3 = (s32[3,1024]{1,0:T(4,128)S(1)}, s32[3,1024]{1,0:T(4,128)}, u32[]{:S(2)}) copy-start(s32[3,1024]{1,0:T(4,128)} %param.4) | copy-start | bytes 36868
  35.9 143.0 %all-gather.2.cloned.1.call-start = ((), (), s32[]{:S(2)}) async-start(), calls=%async_computation.2 | async-start | bytes 8650752 | tf_op jit(solution)/shard_map/all_gather | solution.py:159
  178.9 3.4 %copy-start.1 = (bf16[8192,512]{1,0:T(8,128)(2,1)S(1)}, bf16[8192,512]{1,0:T(8,128)(2,1)}, u32[]{:S(2)}) copy-start(bf16[8192,512]{1,0:T(8,128)(2,1)} %all-gather.2.cloned.1.call-done.sketch_ref) | copy-start | bytes 25165828
Sparse Core Ops, SparseCore 0:
  36.0 62.4 reduce-scatter.1
  101.9 76.9 all-gather.1

commit v2 on v1

--- a/solution.py
+++ b/solution.py
@@ -26,7 +26,7 @@
     return 1.0 - s * s, s * c
 
 
-def sketch_kernel(count_ref, points_ref, waves_ref, test_ref, out_ref, turns_ref, lhs_ref):
+def sketch_kernel(dtype, count_ref, points_ref, waves_ref, test_ref, result_ref, turns_ref, lhs_ref, out_ref):
     rows, width = out_ref.shape[0], test_ref.shape[1]
 
     @pl.when(pl.program_id(0) == 0)
@@ -54,6 +54,11 @@
 
     lax.fori_loop(0, (count_ref[0] + TILE - 1) // TILE, block, 0)
 
+    @pl.when(pl.program_id(0) == pl.num_programs(0) - 1)
+    def _():
+        slot = lax.broadcasted_iota(jnp.int32, out_ref.shape, 0)
+        result_ref[...] = jnp.where(slot < count_ref[0], out_ref[...], 0.0).astype(dtype)
+
 
 def adjoint_kernel(scale, counts_ref, waves_ref, points_ref, sketch_ref, out_ref, turns_ref, lhs_ref, rhs_ref):
     modes, width = out_ref.shape[0], sketch_ref.shape[1] // 2
@@ -92,12 +97,12 @@
     return jnp.pad(rows, ((0, DEPTH - rows.shape[0]), (0, 0))).astype(jnp.bfloat16)
 
 
-def sketch_part(count, points, waves, test_block):
+def sketch_part(count, points, waves, test_block, dtype):
     rows, modes, width = points.shape[0], waves.shape[1], test_block.shape[1]
     step = 1024
     return pl.pallas_call(
-        sketch_kernel,
-        out_shape=jax.ShapeDtypeStruct((rows, 2 * width), jnp.float32),
+        functools.partial(sketch_kernel, dtype),
+        out_shape=jax.ShapeDtypeStruct((rows, 2 * width), dtype),
         grid=(modes // step,),
         in_specs=[
             pl.BlockSpec(memory_space=pltpu.SMEM),
@@ -109,6 +114,7 @@
         scratch_shapes=[
             pltpu.VMEM((step // TILE, TILE, TILE), jnp.float32),
             pltpu.VMEM((step // TILE, 2 * TILE, TILE), jnp.bfloat16),
+            pltpu.VMEM((rows, 2 * width), jnp.float32),
         ],
         compiler_params=pltpu.CompilerParams(vmem_limit_bytes=40 * 2**20),
         cost_estimate=pl.CostEstimate(
@@ -142,21 +148,130 @@
     )(counts, waves, points, sketch)
 
 
+def exchange_kernel(
+    scale, part_ref, info_ref, out_ref, all_ref, landed_ref,
+    sum_out, sum_in, z_out, z_in, x_out, x_in, y_out, y_in, core_out, core_in, info_out, info_in,
+):
+    pt, md = lax.axis_index("pt"), lax.axis_index("md")
+    rows = part_ref.shape[0]
+    quarter = rows // 4
+    core, x, y = pt % 2, (pt // 2) % 2, pt // 4
+    core_pt, x_pt, y_pt = pt + 1 - 2 * core, pt + 2 - 4 * x, pt + 4 - 8 * y
+    xy_pt = x_pt + 4 - 8 * y
+
+    def send(source, target, out_sem, in_sem, to_pt, to_md):
+        copy = pltpu.make_async_remote_copy(
+            src_ref=source, dst_ref=target, send_sem=out_sem, recv_sem=in_sem,
+            device_id=(to_pt, to_md), device_id_type=pl.DeviceIdType.MESH,
+        )
+        copy.start()
+        return copy
+
+    def place(slab, part):
+        return out_ref.at[pl.ds(pl.multiple_of(slab * rows + part * quarter, quarter), quarter), :]
+
+    barrier = pltpu.get_barrier_semaphore()
+    for d in range(1, 4):
+        pl.semaphore_signal(
+            barrier, inc=1, device_id=(pt, (md + d) % 4), device_id_type=pl.DeviceIdType.MESH
+        )
+    for d in range(1, 8):
+        pl.semaphore_signal(
+            barrier, inc=1, device_id=((pt + d) % 8, md), device_id_type=pl.DeviceIdType.MESH
+        )
+    pl.semaphore_wait(barrier, 10)
+
+    sums = []
+    for d in (2, 1, 3):
+        to = (md + d) % 4
+        source = part_ref.at[pl.ds(pl.multiple_of(to * quarter, quarter), quarter), :]
+        sums.append(send(source, landed_ref.at[d - 1], sum_out.at[d - 1], sum_in.at[d - 1], pt, to))
+    others = [
+        send(info_ref, all_ref.at[pt], info_out.at[d - 1], info_in.at[d - 1], (pt + d) % 8, md)
+        for d in range(1, 8)
+    ]
+    all_ref[pt] = info_ref[...]
+    for copy in sums:
+        copy.wait_recv()
+    total = part_ref[pl.ds(pl.multiple_of(md * quarter, quarter), quarter), :].astype(jnp.float32)
+    for d in range(3):
+        total = total + landed_ref[d].astype(jnp.float32)
+    place(pt, md)[...] = (total * scale).astype(jnp.bfloat16)
+
+    own = place(pt, md)
+    ups = [send(own, own, z_out.at[d - 1], z_in.at[d - 1], pt, (md + d) % 4) for d in (1, 2, 3)]
+    pieces = [md, (md + 3) % 4, (md + 2) % 4, (md + 1) % 4]
+    over_x, over_y, over_core = [], [], []
+    for d in range(4):
+        if d:
+            ups[d - 1].wait_recv()
+        here = place(pt, pieces[d])
+        over_x.append(send(here, here, x_out.at[d], x_in.at[d], x_pt, md))
+        over_y.append(send(here, here, y_out.at[d], y_in.at[d], y_pt, md))
+        over_core.append(send(here, here, core_out.at[d], core_in.at[d], core_pt, md))
+    forward_x, forward_y = [], []
+    for d in range(4):
+        over_x[d].wait_recv()
+        here = place(x_pt, pieces[d])
+        if d < 2:
+            forward_y.append(send(here, here, y_out.at[4 + d], y_in.at[4 + d], y_pt, md))
+        over_core.append(send(here, here, core_out.at[4 + d], core_in.at[4 + d], core_pt, md))
+        over_y[d].wait_recv()
+        here = place(y_pt, pieces[d])
+        if d >= 2:
+            forward_x.append(send(here, here, x_out.at[2 + d], x_in.at[2 + d], x_pt, md))
+        over_core.append(send(here, here, core_out.at[8 + d], core_in.at[8 + d], core_pt, md))
+    for d in range(4):
+        (forward_y[d] if d < 2 else forward_x[d - 2]).wait_recv()
+        here = place(xy_pt, pieces[d])
+        over_core.append(send(here, here, core_out.at[12 + d], core_in.at[12 + d], core_pt, md))
+    for copy in over_core + others:
+        copy.wait_recv()
+    for copy in sums + others + ups + over_x + over_y + over_core + forward_x + forward_y:
+        copy.wait_send()
+
+
+def exchange(scale, part, info):
+    rows, width = part.shape
+    sems = [n for n in (3, 3, 6, 6, 16, 7) for _ in range(2)]
+    return pl.pallas_call(
+        functools.partial(exchange_kernel, scale),
+        out_shape=(
+            jax.ShapeDtypeStruct((8 * rows, width), jnp.bfloat16),
+            jax.ShapeDtypeStruct((8,) + info.shape, info.dtype),
+        ),
+        in_specs=[pl.BlockSpec(memory_space=pltpu.VMEM)] * 2,
+        out_specs=(pl.BlockSpec(memory_space=pltpu.VMEM),) * 2,
+        scratch_shapes=[pltpu.VMEM((3, rows // 4, width), jnp.bfloat16)]
+        + [pltpu.SemaphoreType.DMA((n,)) for n in sems],
+        compiler_params=pltpu.CompilerParams(
+            collective_id=0, has_side_effects=True, vmem_limit_bytes=24 * 2**20
+        ),
+    )(part, info)
+
+
 def per_device(grid_index, wavenumbers, test_block, slab_counts):
     capacity = grid_index.shape[1]
-    n_pt = lax.axis_size("pt")
+    n_pt, n_md = lax.axis_size("pt"), lax.axis_size("md")
     y_scale = 1.0 / (32.0 * math.sqrt(M))
     w_scale = 1.0 / math.sqrt(capacity * n_pt)
-    counts = lax.all_gather(slab_counts, "pt", tiled=True)
-    all_points = lax.all_gather(grid_index, "pt", axis=1, tiled=True)
     points = padded(grid_index, 1.0)
     waves = padded(wavenumbers, 1.0 / PERIOD)
-    partial_value = sketch_part(slab_counts, points.T, waves, test_block)
-    quarter = lax.psum_scatter(partial_value, "md", scatter_dimension=0, tiled=True)
-    rows = quarter.shape[0]
-    slot = lax.axis_index("md") * rows + jnp.arange(rows, dtype=jnp.int32)
-    quarter = jnp.where((slot < slab_counts[0])[:, None], quarter * y_scale, 0.0).astype(jnp.bfloat16)
-    sketch = lax.all_gather(quarter, ("pt", "md"), tiled=True)
+    if (n_pt, n_md) == (8, 4):
+        part = sketch_part(slab_counts, points.T, waves, test_block, jnp.bfloat16)
+        info = jnp.concatenate(
+            [grid_index, jnp.broadcast_to(slab_counts[:, None], (5, capacity))], axis=0
+        )
+        sketch, gathered = exchange(y_scale, part, info)
+        counts = gathered[:, 3, 0]
+        all_points = gathered[:, :3, :].transpose(1, 0, 2).reshape(3, n_pt * capacity)
+    else:
+        counts = lax.all_gather(slab_counts, "pt", tiled=True)
+        all_points = lax.all_gather(grid_index, "pt", axis=1, tiled=True)
+        part = sketch_part(slab_counts, points.T, waves, test_block, jnp.float32)
+        share = lax.psum_scatter(part, "md", scatter_dimension=0, tiled=True)
+        share = (share * y_scale).astype(jnp.bfloat16)
+        sketch = lax.all_gather(share, ("pt", "md"), tiled=True)
     own = wavenumbers.shape[1] // n_pt
     mine = lax.dynamic_slice_in_dim(waves, lax.axis_index("pt") * own, own, 1)
     return adjoint_part(w_scale, counts, mine.T, padded(all_points, 1.0), sketch, capacity)

time: 230 us -> 165 us (0.72)
  waiting for transfers between devices: 122 us -> 0 us
  Pallas kernels: 58.5 us -> 154 us
  blocking collectives: 16.5 us -> 0 us
  between operations: 14.1 us -> 0.74 us
  local copies, waits for them, and re-layouts: 11.9 us -> 7.06 us
    pallas_call x1 -> x2, Pallas kernels: 20.9 us -> 116 us  [the longest x1 106 us: exchange(): pl.pallas_call(functools.partial(exchange_kernel, scale), out_shape=(jax....]
    reduce_scatter x1 -> x0, waiting for transfers between devices: 62.6 us -> none  [per_device(): lax.psum_scatter(partial_value, 'md', scatter_dimension=0, tiled=True)]
    all_gather x1 -> x0, waiting for transfers between devices: 59.5 us -> none  [per_device(): sketch = lax.all_gather(quarter, ('pt', 'md'), tiled=True)]
    all_gather x1 -> x0, blocking collectives: 8.55 us -> none  [per_device(): all_points = lax.all_gather(grid_index, 'pt', axis=1, tiled=True)]
    unnamed x1 -> x0, blocking collectives: 7.95 us -> none
    unnamed x14 -> x3, local copies, waits for them, and re-layouts: 9.1 us -> 4.29 us
  transfers between devices with their start and end apart: 2 -> 0, of which waited for: 2 -> 0; matrix products, arithmetic and copies ran while one was open for 1% -> 0% of each run, Pallas kernels for 0% -> 0%
where the time goes in v2:
time: 165 us; the launch traced here: 163 us
  Pallas kernels  154 us (93%)
  local copies, waits for them, and re-layouts  7.06 us (4%)
  other arithmetic  1.68 us (1%)
    pallas_call x1, Pallas kernels, exchange(): pl.pallas_call(functools.partial(exchange_kernel, scale), out_shape=(jax....  106 us
    pallas_call x1, Pallas kernels, adjoint_part(): pl.pallas_call(functools.partial(adjoint_kernel, scale), out_shape=jax.Sh...  37.4 us
    pallas_call x1, Pallas kernels, sketch_part(): pl.pallas_call(functools.partial(sketch_kernel, dtype), out_shape=jax.Sha...  10.2 us
    unnamed x3, local copies, waits for them, and re-layouts  4.29 us

profile of v2, /device:TPU:16, one launch (start us, length us, event | category | flops | bytes accessed | tf_op | source)
XLA Modules:
  0.0 163.1 jit_solution(882681540969582489)
XLA Ops:
  0.7 0.7 convert_convert_fusion.1
  1.4 0.7 concatenate.3.info_ref
  2.1 0.9 multiply_convert_fusion
  3.0 0.2 copy.13
  3.2 0.1 pad_bitcast_fusion.points_ref
  3.3 1.1 copy.14
  4.4 0.9 copy.16
  5.3 0.1 dynamic-slice_bitcast_fusion.waves_ref
  5.4 0.2 pad.16.clone.waves_ref
  5.6 0.0 copy-start
  5.6 3.4 %copy-done = s32[8192,256]{1,0:T(8,128)S(1)} copy-done((s32[8192,256]{1,0:T(8,128)S(1)}, s32[8192,256]{1,0:T(8,128)}, u32[]{:S(2)}) %copy-start) | copy-done | bytes 8388632
  9.0 10.2 %shard_map.46.part_ref = bf16[1024,512]{1,0:T(8,128)(2,1)S(1)} custom-call(s32[1]{0:T(128)} %copy.17.count_ref, bf16[1024,128]{1,0:T(8,128)(2,1)S(1)} %pad_bitcast_fusion.points_ref, bf16[128,8192]{1,0:T(8,128)(2,1)S(1)} %pad.16.clone.waves_ref, s32[8192,256]{1,0:T(8,128)S(1)} %copy-done), custom_call_target="tpu_custom_call" | custom-call | flops 8589934592 | bytes 8388608 | tf_op jit(solution)/shard_map/pallas_call | solution.py:103
  19.2 106.0 %shard_map.47 = (bf16[8192,512]{1,0:T(8,128)(2,1)S(1)}, s32[8,8,1024]{2,1,0:T(8,128)S(1)}) custom-call(bf16[1024,512]{1,0:T(8,128)(2,1)S(1)} %shard_map.46.part_ref, s32[8,1024]{1,0:T(8,128)S(1)} %concatenate.3.info_ref), custom_call_target="tpu_custom_call" | custom-call | tf_op jit(solution)/shard_map/pallas_call | solution.py:237
  125.2 0.2 slice_reduce_fusion.counts_ref
  125.5 0.2 pad.17.points_ref
  125.7 37.4 %shard_map.48 = f32[1024,512]{1,0:T(8,128)} custom-call(s32[8]{0:T(128)S(1)} %slice_reduce_fusion.counts_ref, bf16[1024,128]{1,0:T(8,128)(2,1)S(1)} %dynamic-slice_bitcast_fusion.waves_ref, bf16[128,8192]{1,0:T(8,128)(2,1)S(1)} %pad.17.points_ref, bf16[8192,512]{1,0:T(8,128)(2,1)S(1)} %get-tuple-element.8.sketch_ref), custom_call_target="tpu_custom_call" | custom-call | flops 17179869184 | bytes 8388608 | tf_op jit(solution)/shard_map/pallas_call | solution.py:128
  (1 shorter events, 0.0 us)
Async XLA Ops:
  5.6 3.4 %copy-start = (s32[8192,256]{1,0:T(8,128)S(1)}, s32[8192,256]{1,0:T(8,128)}, u32[]{:S(2)}) copy-start(s32[8192,256]{1,0:T(8,128)} %test_ref.1) | copy-start | bytes 25165828

commit v3 on v2

--- a/solution.py
+++ b/solution.py
@@ -13,6 +13,7 @@
 DEPTH = 128
 TILE = 256
 STRIP = 32
+MARKS = (10, 11, 13, 15, 17, 20, 23, 26, 29)
 
 S = (4.4428679, -7.3074434, 3.59478791, -0.78437358)
 C = (1.41420408, -6.97764202, 5.71523797, -1.72834735)
@@ -90,6 +91,46 @@
     @pl.when(slab == pl.num_programs(0) - 1)
     def _():
         out_ref[...] = out_ref[...] * scale
+
+
+def product_kernel(scale, live_ref, phase_ref, sketch_ref, out_ref, rhs_ref):
+    width = sketch_ref.shape[1] // 2
+    step = pl.program_id(0)
+
+    @pl.when(step == 0)
+    def _():
+        out_ref[...] = jnp.zeros_like(out_ref)
+
+    @pl.when(step < live_ref[0])
+    def _():
+        rhs_ref[pl.ds(0, TILE), :] = sketch_ref[...]
+        rhs_ref[pl.ds(TILE, TILE), pl.ds(0, width)] = sketch_ref[:, pl.ds(width, width)]
+        rhs_ref[pl.ds(TILE, TILE), pl.ds(width, width)] = -sketch_ref[:, pl.ds(0, width)]
+        out_ref[...] += jnp.dot(phase_ref[0], rhs_ref[...], preferred_element_type=jnp.float32)
+
+    @pl.when(step == pl.num_programs(0) - 1)
+    def _():
+        out_ref[...] = out_ref[...] * scale
+
+
+def product(scale, live, order, phase, sketch):
+    blocks, modes, _ = phase.shape
+    width = sketch.shape[1]
+    return pl.pallas_call(
+        lambda live_ref, order_ref, *refs: product_kernel(scale, live_ref, *refs),
+        out_shape=jax.ShapeDtypeStruct((modes, width), jnp.float32),
+        grid_spec=pltpu.PrefetchScalarGridSpec(
+            num_scalar_prefetch=2,
+            grid=(blocks,),
+            in_specs=[
+                pl.BlockSpec((1, modes, 2 * TILE), lambda b, live, order: (order[b], 0, 0)),
+                pl.BlockSpec((TILE, width), lambda b, live, order: (order[b], 0)),
+            ],
+            out_specs=pl.BlockSpec((modes, width), lambda b, live, order: (0, 0)),
+            scratch_shapes=[pltpu.VMEM((2 * TILE, width), jnp.bfloat16)],
+        ),
+        compiler_params=pltpu.CompilerParams(vmem_limit_bytes=24 * 2**20),
+    )(live, order, phase, sketch)
 
 
 def padded(rows, factor):
@@ -149,7 +190,7 @@
 
 
 def exchange_kernel(
-    scale, part_ref, info_ref, out_ref, all_ref, landed_ref,
+    scale, part_ref, info_ref, waves_ref, out_ref, all_ref, phase_ref, landed_ref, points_ref, turns_ref, made_ref, made_sem,
     sum_out, sum_in, z_out, z_in, x_out, x_in, y_out, y_in, core_out, core_in, info_out, info_in,
 ):
     pt, md = lax.axis_index("pt"), lax.axis_index("md")
@@ -191,6 +232,40 @@
         for d in range(1, 8)
     ]
     all_ref[pt] = info_ref[...]
+    for copy in others:
+        copy.wait_recv()
+    points_ref[...] = jnp.zeros_like(points_ref)
+    for slab in range(8):
+        points_ref[pl.ds(0, 8), pl.ds(slab * rows, rows)] = all_ref[slab].astype(jnp.float32)
+
+    def keep(index):
+        slot = index % 2
+        return pltpu.make_async_copy(made_ref.at[slot], phase_ref.at[index], made_sem.at[slot])
+
+    def make(first, last):
+        def body(index, carry):
+            slot = index % 2
+            start = pl.multiple_of(index * TILE, TILE)
+            coords = points_ref[:, pl.ds(start, TILE)].astype(jnp.bfloat16)
+
+            if first >= 2:
+                keep(index - 2).wait()
+            for k in range(waves_ref.shape[0] // TILE):
+                turns_ref[k] = jnp.dot(
+                    waves_ref[pl.ds(k * TILE, TILE), :], coords, preferred_element_type=jnp.float32
+                )
+                for j in range(TILE // STRIP):
+                    re, im = phases(turns_ref[k, pl.ds(j * STRIP, STRIP), :])
+                    at = pl.ds(k * TILE + j * STRIP, STRIP)
+                    made_ref[slot, at, pl.ds(0, TILE)] = re.astype(jnp.bfloat16)
+                    made_ref[slot, at, pl.ds(TILE, TILE)] = im.astype(jnp.bfloat16)
+            keep(index).start()
+            return carry
+
+        lax.fori_loop(first, last, body, 0)
+
+    make(0, 2)
+    make(2, MARKS[0])
     for copy in sums:
         copy.wait_recv()
     total = part_ref[pl.ds(pl.multiple_of(md * quarter, quarter), quarter), :].astype(jnp.float32)
@@ -209,6 +284,7 @@
         over_x.append(send(here, here, x_out.at[d], x_in.at[d], x_pt, md))
         over_y.append(send(here, here, y_out.at[d], y_in.at[d], y_pt, md))
         over_core.append(send(here, here, core_out.at[d], core_in.at[d], core_pt, md))
+        make(MARKS[d], MARKS[d + 1])
     forward_x, forward_y = [], []
     for d in range(4):
         over_x[d].wait_recv()
@@ -221,33 +297,45 @@
         if d >= 2:
             forward_x.append(send(here, here, x_out.at[2 + d], x_in.at[2 + d], x_pt, md))
         over_core.append(send(here, here, core_out.at[8 + d], core_in.at[8 + d], core_pt, md))
+        make(MARKS[4 + d], MARKS[5 + d])
     for d in range(4):
         (forward_y[d] if d < 2 else forward_x[d - 2]).wait_recv()
         here = place(xy_pt, pieces[d])
         over_core.append(send(here, here, core_out.at[12 + d], core_in.at[12 + d], core_pt, md))
-    for copy in over_core + others:
+    make(MARKS[8], phase_ref.shape[0])
+    keep(phase_ref.shape[0] - 2).wait()
+    keep(phase_ref.shape[0] - 1).wait()
+    for copy in over_core:
         copy.wait_recv()
     for copy in sums + others + ups + over_x + over_y + over_core + forward_x + forward_y:
         copy.wait_send()
 
 
-def exchange(scale, part, info):
+def exchange(scale, part, info, waves):
     rows, width = part.shape
+    modes = waves.shape[0]
     sems = [n for n in (3, 3, 6, 6, 16, 7) for _ in range(2)]
     return pl.pallas_call(
         functools.partial(exchange_kernel, scale),
         out_shape=(
             jax.ShapeDtypeStruct((8 * rows, width), jnp.bfloat16),
             jax.ShapeDtypeStruct((8,) + info.shape, info.dtype),
-        ),
-        in_specs=[pl.BlockSpec(memory_space=pltpu.VMEM)] * 2,
-        out_specs=(pl.BlockSpec(memory_space=pltpu.VMEM),) * 2,
-        scratch_shapes=[pltpu.VMEM((3, rows // 4, width), jnp.bfloat16)]
+            jax.ShapeDtypeStruct((8 * rows // TILE, modes, 2 * TILE), jnp.bfloat16),
+        ),
+        in_specs=[pl.BlockSpec(memory_space=pltpu.VMEM)] * 3,
+        out_specs=(pl.BlockSpec(memory_space=pltpu.VMEM),) * 2 + (pl.BlockSpec(memory_space=pl.ANY),),
+        scratch_shapes=[
+            pltpu.VMEM((3, rows // 4, width), jnp.bfloat16),
+            pltpu.VMEM((DEPTH, 8 * rows), jnp.float32),
+            pltpu.VMEM((modes // TILE, TILE, TILE), jnp.float32),
+            pltpu.VMEM((2, modes, 2 * TILE), jnp.bfloat16),
+            pltpu.SemaphoreType.DMA((2,)),
+        ]
         + [pltpu.SemaphoreType.DMA((n,)) for n in sems],
         compiler_params=pltpu.CompilerParams(
-            collective_id=0, has_side_effects=True, vmem_limit_bytes=24 * 2**20
-        ),
-    )(part, info)
+            collective_id=0, has_side_effects=True, vmem_limit_bytes=32 * 2**20
+        ),
+    )(part, info, waves)
 
 
 def per_device(grid_index, wavenumbers, test_block, slab_counts):
@@ -257,14 +345,21 @@
     w_scale = 1.0 / math.sqrt(capacity * n_pt)
     points = padded(grid_index, 1.0)
     waves = padded(wavenumbers, 1.0 / PERIOD)
+    own = wavenumbers.shape[1] // n_pt
+    mine = lax.dynamic_slice_in_dim(waves, lax.axis_index("pt") * own, own, 1)
     if (n_pt, n_md) == (8, 4):
         part = sketch_part(slab_counts, points.T, waves, test_block, jnp.bfloat16)
         info = jnp.concatenate(
             [grid_index, jnp.broadcast_to(slab_counts[:, None], (5, capacity))], axis=0
         )
-        sketch, gathered = exchange(y_scale, part, info)
-        counts = gathered[:, 3, 0]
-        all_points = gathered[:, :3, :].transpose(1, 0, 2).reshape(3, n_pt * capacity)
+        sketch, gathered, phase = exchange(y_scale, part, info, mine.T)
+        per_slab = (gathered[:, 3, 0] + TILE - 1) // TILE
+        ends = jnp.sum(jnp.where(jnp.arange(8)[:, None] <= jnp.arange(8)[None, :], per_slab[:, None], 0), axis=0)
+        nth = jnp.minimum(jnp.arange(phase.shape[0], dtype=jnp.int32), ends[7] - 1)
+        past = (ends[None, :] <= nth[:, None]).astype(jnp.int32)
+        slab = jnp.sum(past, axis=1)
+        order = slab * (capacity // TILE) + nth - jnp.sum(past * per_slab[None, :], axis=1)
+        return product(w_scale, ends[7:], order.astype(jnp.int32), phase, sketch)
     else:
         counts = lax.all_gather(slab_counts, "pt", tiled=True)
         all_points = lax.all_gather(grid_index, "pt", axis=1, tiled=True)
@@ -272,8 +367,6 @@
         share = lax.psum_scatter(part, "md", scatter_dimension=0, tiled=True)
         share = (share * y_scale).astype(jnp.bfloat16)
         sketch = lax.all_gather(share, ("pt", "md"), tiled=True)
-    own = wavenumbers.shape[1] // n_pt
-    mine = lax.dynamic_slice_in_dim(waves, lax.axis_index("pt") * own, own, 1)
     return adjoint_part(w_scale, counts, mine.T, padded(all_points, 1.0), sketch, capacity)
 
 

time: 165 us -> 157 us (0.952); the launches traced: 163 us -> 157 us
  Pallas kernels: 154 us -> 146 us
    pallas_call x1, Pallas kernels: 37.4 us -> 27.2 us  [product(): pl.pallas_call(lambda live_ref, order_ref, *refs: product_kernel(scale, l...]
    pallas_call x1, Pallas kernels: 10.2 us -> 19.8 us  [sketch_part(): pl.pallas_call(functools.partial(sketch_kernel, dtype), out_shape=jax.Sha...]
    pallas_call x1, Pallas kernels: 106 us -> 99 us  [exchange(): pl.pallas_call(functools.partial(exchange_kernel, scale), out_shape=(jax....]
where the time goes in v3:
time: 157 us
  Pallas kernels  146 us (93%)
  local copies, waits for them, and re-layouts  7.26 us (5%)
  other arithmetic  2.1 us (1%)
    pallas_call x1, Pallas kernels, exchange(): pl.pallas_call(functools.partial(exchange_kernel, scale), out_shape=(jax....  99 us
    pallas_call x1, Pallas kernels, product(): pl.pallas_call(lambda live_ref, order_ref, *refs: product_kernel(scale, l...  27.2 us
    pallas_call x1, Pallas kernels, sketch_part(): pl.pallas_call(functools.partial(sketch_kernel, dtype), out_shape=jax.Sha...  19.8 us
    unnamed x3, local copies, waits for them, and re-layouts  4.29 us

profile of v3, /device:TPU:16, one launch (start us, length us, event | category | flops | bytes accessed | tf_op | source)
XLA Modules:
  0.0 156.7 jit_solution(16921464603602672680)
XLA Ops:
  0.7 0.7 convert_convert_fusion
  1.4 0.7 concatenate.3.info_ref
  2.1 0.9 multiply_convert_fusion
  3.0 0.2 copy.17
  3.2 0.1 pad_bitcast_fusion.points_ref
  3.3 1.1 copy.18
  4.4 0.9 copy.20
  5.3 0.1 dynamic-slice_bitcast_fusion.waves_ref
  5.4 0.2 pad.12.clone.waves_ref
  5.6 0.0 copy-start
  5.6 3.4 %copy-done = s32[8192,256]{1,0:T(8,128)S(1)} copy-done((s32[8192,256]{1,0:T(8,128)S(1)}, s32[8192,256]{1,0:T(8,128)}, u32[]{:S(2)}) %copy-start) | copy-done | bytes 8388632
  9.0 19.8 %shard_map.46.part_ref = bf16[1024,512]{1,0:T(8,128)(2,1)S(1)} custom-call(s32[1]{0:T(128)} %copy.21.count_ref, bf16[1024,128]{1,0:T(8,128)(2,1)S(1)} %pad_bitcast_fusion.points_ref, bf16[128,8192]{1,0:T(8,128)(2,1)S(1)} %pad.12.clone.waves_ref, s32[8192,256]{1,0:T(8,128)S(1)} %copy-done), custom_call_target="tpu_custom_call" | custom-call | flops 8589934592 | bytes 8388608 | tf_op jit(solution)/shard_map/pallas_call | solution.py:144
  28.7 99.0 %shard_map.47 = (bf16[8192,512]{1,0:T(8,128)(2,1)S(1)}, s32[8,8,1024]{2,1,0:T(8,128)S(1)}, bf16[32,1024,512]{2,1,0:T(8,128)(2,1)}) custom-call(bf16[1024,512]{1,0:T(8,128)(2,1)S(1)} %shard_map.46.part_ref, s32[8,1024]{1,0:T(8,128)S(1)} %concatenate.3.info_ref, bf16[1024,128]{1,0:T(8,128)(2,1)S(1)} %dynamic-slice_bitcast_fusion.waves_ref), custom_call_target="tpu_custom_call" | custom-call | tf_op jit(solution)/shard_map/pallas_call | solution.py:318
  127.8 0.2 add_reduce_fusion
  128.0 0.1 select_reduce_fusion
  128.1 0.7 slice.8.live_ref
  129.4 0.1 fusion
  129.6 27.2 %shard_map.48 = f32[1024,512]{1,0:T(8,128)} custom-call(s32[1]{0:T(128)} %slice.8.live_ref, s32[32]{0:T(128)S(1)} %add_subtract_fusion.order_ref, bf16[32,1024,512]{2,1,0:T(8,128)(2,1)} %get-tuple-element.9.refs_0_, bf16[8192,512]{1,0:T(8,128)(2,1)S(1)} %get-tuple-element.10.refs_1_), custom_call_target="tpu_custom_call" | custom-call | tf_op jit(solution)/shard_map/pallas_call | solution.py:119
  (3 shorter events, 0.0 us)
Async XLA Ops:
  5.6 3.4 %copy-start = (s32[8192,256]{1,0:T(8,128)S(1)}, s32[8192,256]{1,0:T(8,128)}, u32[]{:S(2)}) copy-start(s32[8192,256]{1,0:T(8,128)} %test_ref.1) | copy-start | bytes 25165828

commit v4 on v3

--- a/solution.py
+++ b/solution.py
@@ -13,6 +13,7 @@
 DEPTH = 128
 TILE = 256
 STRIP = 32
+SKETCH = (2048, 512, 512)
 MARKS = (10, 11, 13, 15, 17, 20, 23, 26, 29)
 
 S = (4.4428679, -7.3074434, 3.59478791, -0.78437358)
@@ -27,33 +28,35 @@
     return 1.0 - s * s, s * c
 
 
-def sketch_kernel(dtype, count_ref, points_ref, waves_ref, test_ref, result_ref, turns_ref, lhs_ref, out_ref):
-    rows, width = out_ref.shape[0], test_ref.shape[1]
+def sketch_kernel(
+    dtype, count_ref, points_ref, waves_ref, test_ref, result_ref, turns_ref, lhs_ref, out_ref, cast_ref
+):
+    width, tile, step = test_ref.shape[1], turns_ref.shape[1], test_ref.shape[0]
+    chunk = turns_ref.shape[2]
 
     @pl.when(pl.program_id(0) == 0)
     def _():
         out_ref[...] = jnp.zeros_like(out_ref)
 
+    cast_ref[...] = test_ref[...].astype(jnp.float32).astype(jnp.bfloat16)
+
     def block(index, carry):
-        first = pl.multiple_of(index * TILE, TILE)
-        total = None
-        for k in range(test_ref.shape[0] // TILE):
-            cols = pl.ds(k * TILE, TILE)
+        first = pl.multiple_of(index * tile, tile)
+        for k in range(step // chunk):
+            cols = pl.ds(k * chunk, chunk)
             turns_ref[k] = jnp.dot(
-                points_ref[pl.ds(first, TILE), :], waves_ref[:, cols], preferred_element_type=jnp.float32
+                points_ref[pl.ds(first, tile), :], waves_ref[:, cols], preferred_element_type=jnp.float32
             )
-            for j in range(TILE // STRIP):
+            for j in range(tile // STRIP):
                 re, im = phases(turns_ref[k, pl.ds(j * STRIP, STRIP), :])
-                lhs_ref[k, pl.ds(j * STRIP, STRIP), :] = re.astype(jnp.bfloat16)
-                lhs_ref[k, pl.ds(TILE + j * STRIP, STRIP), :] = im.astype(jnp.bfloat16)
-            test = test_ref[cols, :].astype(jnp.float32).astype(jnp.bfloat16)
-            part = jnp.dot(lhs_ref[k], test, preferred_element_type=jnp.float32)
-            total = part if total is None else total + part
-        out_ref[pl.ds(first, TILE), pl.ds(0, width)] += total[:TILE]
-        out_ref[pl.ds(first, TILE), pl.ds(width, width)] += total[TILE:]
+                lhs_ref[pl.ds(j * STRIP, STRIP), cols] = re.astype(jnp.bfloat16)
+                lhs_ref[pl.ds(tile + j * STRIP, STRIP), cols] = im.astype(jnp.bfloat16)
+        total = jnp.dot(lhs_ref[...], cast_ref[...], preferred_element_type=jnp.float32)
+        out_ref[pl.ds(first, tile), pl.ds(0, width)] += total[:tile]
+        out_ref[pl.ds(first, tile), pl.ds(width, width)] += total[tile:]
         return carry
 
-    lax.fori_loop(0, (count_ref[0] + TILE - 1) // TILE, block, 0)
+    lax.fori_loop(0, (count_ref[0] + tile - 1) // tile, block, 0)
 
     @pl.when(pl.program_id(0) == pl.num_programs(0) - 1)
     def _():
@@ -93,20 +96,24 @@
         out_ref[...] = out_ref[...] * scale
 
 
-def product_kernel(scale, live_ref, phase_ref, sketch_ref, out_ref, rhs_ref):
-    width = sketch_ref.shape[1] // 2
+def product_kernel(scale, live_ref, first_ref, second_ref, upper_ref, lower_ref, out_ref, rhs_ref):
+    width = upper_ref.shape[1] // 2
     step = pl.program_id(0)
 
     @pl.when(step == 0)
     def _():
         out_ref[...] = jnp.zeros_like(out_ref)
 
-    @pl.when(step < live_ref[0])
-    def _():
-        rhs_ref[pl.ds(0, TILE), :] = sketch_ref[...]
-        rhs_ref[pl.ds(TILE, TILE), pl.ds(0, width)] = sketch_ref[:, pl.ds(width, width)]
-        rhs_ref[pl.ds(TILE, TILE), pl.ds(width, width)] = -sketch_ref[:, pl.ds(0, width)]
-        out_ref[...] += jnp.dot(phase_ref[0], rhs_ref[...], preferred_element_type=jnp.float32)
+    @pl.when(2 * step < live_ref[0])
+    def _():
+        upper, lower = upper_ref[...], lower_ref[...]
+        lower = jnp.where(2 * step + 1 < live_ref[0], lower, jnp.zeros_like(lower))
+        for g, rows in enumerate((upper, lower)):
+            rhs_ref[pl.ds(2 * g * TILE, TILE), :] = rows
+            rhs_ref[pl.ds((2 * g + 1) * TILE, TILE), pl.ds(0, width)] = rows[:, width:]
+            rhs_ref[pl.ds((2 * g + 1) * TILE, TILE), pl.ds(width, width)] = -rows[:, :width]
+        lhs = jnp.concatenate([first_ref[0], second_ref[0]], axis=1)
+        out_ref[...] += jnp.dot(lhs, rhs_ref[...], preferred_element_type=jnp.float32)
 
     @pl.when(step == pl.num_programs(0) - 1)
     def _():
@@ -121,16 +128,18 @@
         out_shape=jax.ShapeDtypeStruct((modes, width), jnp.float32),
         grid_spec=pltpu.PrefetchScalarGridSpec(
             num_scalar_prefetch=2,
-            grid=(blocks,),
+            grid=(blocks // 2,),
             in_specs=[
-                pl.BlockSpec((1, modes, 2 * TILE), lambda b, live, order: (order[b], 0, 0)),
-                pl.BlockSpec((TILE, width), lambda b, live, order: (order[b], 0)),
+                pl.BlockSpec((1, modes, 2 * TILE), lambda b, live, order: (order[2 * b], 0, 0)),
+                pl.BlockSpec((1, modes, 2 * TILE), lambda b, live, order: (order[2 * b + 1], 0, 0)),
+                pl.BlockSpec((TILE, width), lambda b, live, order: (order[2 * b], 0)),
+                pl.BlockSpec((TILE, width), lambda b, live, order: (order[2 * b + 1], 0)),
             ],
             out_specs=pl.BlockSpec((modes, width), lambda b, live, order: (0, 0)),
-            scratch_shapes=[pltpu.VMEM((2 * TILE, width), jnp.bfloat16)],
-        ),
-        compiler_params=pltpu.CompilerParams(vmem_limit_bytes=24 * 2**20),
-    )(live, order, phase, sketch)
+            scratch_shapes=[pltpu.VMEM((4 * TILE, width), jnp.bfloat16)],
+        ),
+        compiler_params=pltpu.CompilerParams(vmem_limit_bytes=30 * 2**20),
+    )(live, order, phase, phase, sketch, sketch)
 
 
 def padded(rows, factor):
@@ -140,7 +149,7 @@
 
 def sketch_part(count, points, waves, test_block, dtype):
     rows, modes, width = points.shape[0], waves.shape[1], test_block.shape[1]
-    step = 1024
+    step, tile, chunk = SKETCH
     return pl.pallas_call(
         functools.partial(sketch_kernel, dtype),
         out_shape=jax.ShapeDtypeStruct((rows, 2 * width), dtype),
@@ -153,9 +162,10 @@
         ],
         out_specs=pl.BlockSpec((rows, 2 * width), lambda m: (0, 0)),
         scratch_shapes=[
-            pltpu.VMEM((step // TILE, TILE, TILE), jnp.float32),
-            pltpu.VMEM((step // TILE, 2 * TILE, TILE), jnp.bfloat16),
+            pltpu.VMEM((step // chunk, tile, chunk), jnp.float32),
+            pltpu.VMEM((2 * tile, step), jnp.bfloat16),
             pltpu.VMEM((rows, 2 * width), jnp.float32),
+            pltpu.VMEM((step, width), jnp.bfloat16),
         ],
         compiler_params=pltpu.CompilerParams(vmem_limit_bytes=40 * 2**20),
         cost_estimate=pl.CostEstimate(

time: 157 us -> 137 us (0.87)
  Pallas kernels: 146 us -> 126 us
    pallas_call x1, Pallas kernels: 27.2 us -> 20.1 us  [product(): pl.pallas_call(lambda live_ref, order_ref, *refs: product_kernel(scale, l...]
    pallas_call x1, Pallas kernels: 99 us -> 92.4 us  [exchange(): pl.pallas_call(functools.partial(exchange_kernel, scale), out_shape=(jax....]
    pallas_call x1, Pallas kernels: 19.8 us -> 13.4 us  [sketch_part(): pl.pallas_call(functools.partial(sketch_kernel, dtype), out_shape=jax.Sha...]
where the time goes in v4:
time: 137 us
  Pallas kernels  126 us (92%)
  local copies, waits for them, and re-layouts  7.26 us (5%)
  other arithmetic  2.1 us (2%)
  between operations  1.42 us (1%)
    pallas_call x1, Pallas kernels, exchange(): pl.pallas_call(functools.partial(exchange_kernel, scale), out_shape=(jax....  92.4 us
    pallas_call x1, Pallas kernels, product(): pl.pallas_call(lambda live_ref, order_ref, *refs: product_kernel(scale, l...  20.1 us
    pallas_call x1, Pallas kernels, sketch_part(): pl.pallas_call(functools.partial(sketch_kernel, dtype), out_shape=jax.Sha...  13.4 us
    unnamed x3, local copies, waits for them, and re-layouts  4.29 us

profile of v4, /device:TPU:16, one launch (start us, length us, event | category | flops | bytes accessed | tf_op | source)
XLA Modules:
  0.0 136.7 jit_solution(2756578823187275188)
XLA Ops:
  0.7 0.7 convert_convert_fusion
  1.4 0.7 concatenate.3.info_ref
  2.1 0.9 multiply_convert_fusion
  3.0 0.2 copy.17
  3.2 0.1 pad_bitcast_fusion.points_ref
  3.3 1.1 copy.18
  4.4 0.9 copy.20
  5.3 0.1 dynamic-slice_bitcast_fusion.waves_ref
  5.4 0.2 pad.12.clone.waves_ref
  5.6 0.0 copy-start
  5.6 3.4 %copy-done = s32[8192,256]{1,0:T(8,128)S(1)} copy-done((s32[8192,256]{1,0:T(8,128)S(1)}, s32[8192,256]{1,0:T(8,128)}, u32[]{:S(2)}) %copy-start) | copy-done | bytes 8388632
  9.0 13.4 %shard_map.46.part_ref = bf16[1024,512]{1,0:T(8,128)(2,1)S(1)} custom-call(s32[1]{0:T(128)} %copy.21.count_ref, bf16[1024,128]{1,0:T(8,128)(2,1)S(1)} %pad_bitcast_fusion.points_ref, bf16[128,8192]{1,0:T(8,128)(2,1)S(1)} %pad.12.clone.waves_ref, s32[8192,256]{1,0:T(8,128)S(1)} %copy-done), custom_call_target="tpu_custom_call" | custom-call | flops 8589934592 | bytes 8388608 | tf_op jit(solution)/shard_map/pallas_call | solution.py:153
  22.4 92.4 %shard_map.47 = (bf16[8192,512]{1,0:T(8,128)(2,1)S(1)}, s32[8,8,1024]{2,1,0:T(8,128)S(1)}, bf16[32,1024,512]{2,1,0:T(8,128)(2,1)}) custom-call(bf16[1024,512]{1,0:T(8,128)(2,1)S(1)} %shard_map.46.part_ref, s32[8,1024]{1,0:T(8,128)S(1)} %concatenate.3.info_ref, bf16[1024,128]{1,0:T(8,128)(2,1)S(1)} %dynamic-slice_bitcast_fusion.waves_ref), custom_call_target="tpu_custom_call" | custom-call | tf_op jit(solution)/shard_map/pallas_call | solution.py:328
  114.8 0.2 add_reduce_fusion
  115.1 0.1 select_reduce_fusion
  115.1 0.7 slice.8.live_ref
  116.5 0.1 fusion
  116.6 20.1 %shard_map.48 = f32[1024,512]{1,0:T(8,128)} custom-call(s32[1]{0:T(128)} %slice.8.live_ref, s32[32]{0:T(128)S(1)} %add_subtract_fusion.order_ref, bf16[32,1024,512]{2,1,0:T(8,128)(2,1)} %get-tuple-element.9.refs_0_.refs_1_, bf16[32,1024,512]{2,1,0:T(8,128)(2,1)} %get-tuple-element.9.refs_0_.refs_1_, bf16[8192,512]{1,0:T(8,128)(2,1)S(1)} %get-tuple-element.10.refs_2_.refs_3_, ...), custom_call_target="tpu_custom_call" | custom-call | tf_op jit(solution)/shard_map/pallas_call | solution.py:126
  (3 shorter events, 0.0 us)
Async XLA Ops:
  5.6 3.4 %copy-start = (s32[8192,256]{1,0:T(8,128)S(1)}, s32[8192,256]{1,0:T(8,128)}, u32[]{:S(2)}) copy-start(s32[8192,256]{1,0:T(8,128)} %test_ref.1) | copy-start | bytes 25165828

commit v5 on v4

--- a/solution.py
+++ b/solution.py
@@ -167,7 +167,7 @@
             pltpu.VMEM((rows, 2 * width), jnp.float32),
             pltpu.VMEM((step, width), jnp.bfloat16),
         ],
-        compiler_params=pltpu.CompilerParams(vmem_limit_bytes=40 * 2**20),
+        compiler_params=pltpu.CompilerParams(vmem_limit_bytes=58 * 2**20),
         cost_estimate=pl.CostEstimate(
             flops=4 * rows * modes * width, bytes_accessed=4 * modes * width, transcendentals=0
         ),

time: 137 us -> 142 us (1.036)
  Pallas kernels: 126 us -> 130 us
    pallas_call x1, Pallas kernels: 13.4 us -> 16.2 us  [sketch_part(): pl.pallas_call(functools.partial(sketch_kernel, dtype), out_shape=jax.Sha...]
    unnamed x3, local copies, waits for them, and re-layouts: 4.29 us -> 2.14 us
where the time goes in v5:
time: 142 us; the launch traced here: 140 us
  Pallas kernels  130 us (92%)
  local copies, waits for them, and re-layouts  7.13 us (5%)
  other arithmetic  2.1 us (1%)
    pallas_call x1, Pallas kernels, exchange(): pl.pallas_call(functools.partial(exchange_kernel, scale), out_shape=(jax....  92 us
    pallas_call x1, Pallas kernels, product(): pl.pallas_call(lambda live_ref, order_ref, *refs: product_kernel(scale, l...  21.5 us
    pallas_call x1, Pallas kernels, sketch_part(): pl.pallas_call(functools.partial(sketch_kernel, dtype), out_shape=jax.Sha...  16.2 us

profile of v5, /device:TPU:16, one launch (start us, length us, event | category | flops | bytes accessed | tf_op | source)
XLA Modules:
  0.0 140.3 jit_solution(15396787286480809139)
XLA Ops:
  0.7 0.7 convert_convert_fusion
  1.4 0.7 concatenate.3.info_ref
  2.1 0.9 multiply_convert_fusion
  3.0 0.2 copy.17
  3.2 0.8 pad_bitcast_fusion.points_ref
  4.0 1.0 copy.18
  5.1 0.9 copy.20
  6.0 0.1 dynamic-slice_bitcast_fusion.waves_ref
  6.1 1.5 %pad.12.clone.waves_ref = bf16[128,8192]{1,0:T(8,128)(2,1)} pad(bf16[3,8192]{1,0:T(4,128)(2,1)S(1)} %copy.20, bf16[]{:T(256)} %constant.31.clone.1), padding=0_125x0_0 | pad | bytes 2146306 | tf_op jit(solution)/shard_map/jit(_pad)/pad | solution.py:147
  7.6 16.2 %shard_map.46.part_ref = bf16[1024,512]{1,0:T(8,128)(2,1)} custom-call(s32[1]{0:T(128)} %copy.21.count_ref, bf16[1024,128]{1,0:T(8,128)(2,1)} %pad_bitcast_fusion.points_ref, bf16[128,8192]{1,0:T(8,128)(2,1)} %pad.12.clone.waves_ref, s32[8192,256]{1,0:T(8,128)} %test_ref.1), custom_call_target="tpu_custom_call" | custom-call | flops 8589934592 | bytes 8388608 | tf_op jit(solution)/shard_map/pallas_call | solution.py:153
  23.8 0.0 copy-start
  23.8 1.2 copy-done
  25.0 92.0 %shard_map.47 = (bf16[8192,512]{1,0:T(8,128)(2,1)S(1)}, s32[8,8,1024]{2,1,0:T(8,128)S(1)}, bf16[32,1024,512]{2,1,0:T(8,128)(2,1)}) custom-call(bf16[1024,512]{1,0:T(8,128)(2,1)S(1)} %copy-done, s32[8,1024]{1,0:T(8,128)S(1)} %concatenate.3.info_ref, bf16[1024,128]{1,0:T(8,128)(2,1)S(1)} %dynamic-slice_bitcast_fusion.waves_ref), custom_call_target="tpu_custom_call" | custom-call | tf_op jit(solution)/shard_map/pallas_call | solution.py:328
  117.0 0.2 add_reduce_fusion
  117.3 0.1 select_reduce_fusion
  117.4 0.7 slice.8.live_ref
  118.7 0.1 fusion
  118.8 21.5 %shard_map.48 = f32[1024,512]{1,0:T(8,128)} custom-call(s32[1]{0:T(128)} %slice.8.live_ref, s32[32]{0:T(128)S(1)} %add_subtract_fusion.order_ref, bf16[32,1024,512]{2,1,0:T(8,128)(2,1)} %get-tuple-element.9.refs_0_.refs_1_, bf16[32,1024,512]{2,1,0:T(8,128)(2,1)} %get-tuple-element.9.refs_0_.refs_1_, bf16[8192,512]{1,0:T(8,128)(2,1)S(1)} %get-tuple-element.10.refs_2_.refs_3_, ...), custom_call_target="tpu_custom_call" | custom-call | tf_op jit(solution)/shard_map/pallas_call | solution.py:126
  (3 shorter events, 0.0 us)
Async XLA Ops:
  23.8 1.2 copy-start
